TPU v7x, 128 devices: a whole 4x4x4 slice. The times are simulated.
128 devices in a mesh: rows: 128 (over z, y, x, core).
Axes of the slice: x: 4, y: 4, z: 4, core: 2. Of those that a mesh axis runs over, the one named last changes fastest.
Arguments:
- edge_tiles: bfloat16 [32768, 128, 128], P('rows'), may hold values from -0.5 to 0.5
- tile_row: int32 [32768], P('rows'), may hold values from 0 to 7
- tile_slot: int32 [32768], P('rows'), may hold values from 0 to 255, as said below
- tile_count: int32 [128], P('rows'), may hold values from 32 to 256, as said below
- fetch_list: int32 [128, 256], P('rows'), may hold values from 0 to 7, as said below
- hub_start: float32 [8, 131072], P(None, 'rows'), may hold values from -6 to 6
Outputs:
- hub: float32 [8, 131072], P(None, 'rows')
- authority: float32 [8, 131072], P(None, 'rows')
Inputs may be any that keep to these rules, and one draw needn't show every extreme that they name: tile_slot[t] = p * 2 + k names entry k of the fetch_list group of device p, in the row of the tile's own device. `fetch_list`: entries p * 2 to p * 2 + 1 of each row are 2 distinct block numbers among device p's own 8 blocks. Tile slots of device d at positions 256 * d + i with i >= tile_count[d] are not part of the graph.
All inputs are finite; a program needn't handle non-finite values.
Results may differ from a plain program's by a relative error of at most 0.004.
Values may be sent and summed in bfloat16 or wider, within the bound.
A program may use at most 64 MiB of HBM per device.

v0:
```python
import functools

import jax
import jax.numpy as jnp
from jax import lax
from jax.sharding import Mesh
from jax.sharding import PartitionSpec as P

ITERS = 2
ROWS = ("rows_0", "rows_1", "rows_2", "rows_3")


def by_axis(x, axes):
    return functools.reduce(lax.psum, axes, x)


def square_sums(raw_blocks):
    return jnp.sum(raw_blocks * raw_blocks, axis=(0, 2))


def rescale(raw_blocks, sums, node_total):
    return raw_blocks / jnp.sqrt(sums / node_total + 1e-06)[None, :, None]


def hub_norm_sum(hub_raw):
    return by_axis(square_sums(hub_raw), ROWS)


def per_device(edge_tiles, tile_row, tile_slot, tile_count, fetch_list, hub_start):
    devices = lax.axis_size(ROWS)
    tile_total = edge_tiles.shape[0]
    tile_edge = edge_tiles.shape[1]
    columns = hub_start.shape[0]
    block_local = hub_start.shape[1] // tile_edge
    slot_total = fetch_list.shape[1]
    slots_each = slot_total // devices
    node_total = hub_start.shape[1] * devices
    group_size = min(64, tile_total)
    live_count = tile_count[0]
    rounds = (live_count + group_size - 1) // group_size
    wanted_local = fetch_list[0]
    block_ids = jnp.arange(block_local, dtype=jnp.int32)

    def group_inputs(group_index):
        first_tile = group_index * group_size
        tiles_now = lax.dynamic_slice_in_dim(edge_tiles, first_tile, group_size, 0)
        rows_now = lax.dynamic_slice_in_dim(tile_row, first_tile, group_size, 0)
        slots_now = lax.dynamic_slice_in_dim(tile_slot, first_tile, group_size, 0)
        alive_mask = (first_tile + jnp.arange(group_size, dtype=jnp.int32) < live_count).astype(
            jnp.float32
        )
        return (tiles_now, rows_now, slots_now, alive_mask)

    owner_wanted = lax.all_to_all(
        wanted_local.reshape(devices, slots_each), ROWS, split_axis=0, concat_axis=0, tiled=True
    ).reshape(slot_total)
    owner_selector = (block_ids[:, None] == owner_wanted[None, :]).astype(jnp.float32)
    hub_blocks = hub_start.reshape(columns, block_local, tile_edge).transpose(1, 0, 2)
    hub_low = hub_blocks.astype(jnp.bfloat16)
    authority_blocks = hub_blocks
    for sweep in range(ITERS):

        def transpose_accumulate(group_index, partial_value):
            tiles_now, rows_now, slots_now, alive_mask = group_inputs(group_index)
            source = jnp.take(hub_low, rows_now, axis=0)
            product = jnp.einsum(
                "gce,gef->gcf", source, tiles_now, preferred_element_type=jnp.float32
            )
            product = product * alive_mask[:, None, None]
            return partial_value + jax.ops.segment_sum(product, slots_now, num_segments=slot_total)

        transpose_start_value = jnp.zeros((slot_total, columns, tile_edge), jnp.float32)
        partial_value = lax.fori_loop(0, rounds, transpose_accumulate, transpose_start_value)
        returned = lax.all_to_all(
            partial_value.reshape(devices, slots_each, columns, tile_edge),
            ROWS,
            split_axis=0,
            concat_axis=0,
            tiled=True,
        )
        returned = returned.reshape(slot_total, columns, tile_edge)
        authority_raw = jnp.einsum(
            "bs,scx->bcx", owner_selector, returned, precision=lax.Precision.HIGHEST
        )
        authority_low = authority_raw.astype(jnp.bfloat16)
        reply = jnp.take(authority_low, owner_wanted, axis=0).reshape(
            devices, slots_each, columns, tile_edge
        )
        fetched = lax.all_to_all(reply, ROWS, split_axis=0, concat_axis=0, tiled=True).reshape(
            slot_total, columns, tile_edge
        )
        final_sweep = sweep + 1 == ITERS
        if final_sweep:
            authority_sums = by_axis(square_sums(authority_raw), ROWS)

        def forward_accumulate(group_index, partial_value):
            tiles_now, rows_now, slots_now, alive_mask = group_inputs(group_index)
            source = jnp.take(fetched, slots_now, axis=0)
            product = jnp.einsum(
                "gcf,gef->gce", source, tiles_now, preferred_element_type=jnp.float32
            )
            selector = (block_ids[:, None] == rows_now[None, :]).astype(jnp.float32) * alive_mask[
                None, :
            ]
            return partial_value + jnp.einsum(
                "bg,gcx->bcx", selector, product, precision=lax.Precision.HIGHEST
            )

        start_value = jnp.zeros((block_local, columns, tile_edge), jnp.float32)
        hub_raw = lax.fori_loop(0, rounds, forward_accumulate, start_value)
        if final_sweep:
            hub_sums = hub_norm_sum(hub_raw)
            authority_blocks = rescale(authority_raw, authority_sums, node_total)
        else:
            hub_sums = hub_norm_sum(hub_raw)
        hub_blocks = rescale(hub_raw, hub_sums, node_total)
        hub_low = hub_blocks.astype(jnp.bfloat16)
    hub = hub_blocks.transpose(1, 0, 2).reshape(columns, block_local * tile_edge)
    authority = authority_blocks.transpose(1, 0, 2).reshape(columns, block_local * tile_edge)
    return (hub, authority)


def solution(mesh):
    split = Mesh(mesh.devices.reshape(4, 4, 4, 2), ("rows_0", "rows_1", "rows_2", "rows_3"))
    placed = (P(ROWS, None, None), P(ROWS), P(ROWS), P(ROWS), P(ROWS, None), P(None, ROWS))
    return jax.shard_map(
        per_device,
        mesh=split,
        in_specs=placed,
        out_specs=(P(None, ROWS), P(None, ROWS)),
        check_vma=False,
    )
```

profile of v0, /device:TPU:1, one launch (start us, length us, event | category | flops | bytes accessed | tf_op | source)
XLA Modules:
  0.0 263.0 jit_solution(7109227219538388047)
XLA Ops:
  1.1 1.3 reduce.6
  2.4 0.8 all_to_all.18
  3.1 11.5 %all-to-all-start = ((s32[128,1,2]{2,1,0:T(1,128)}), s32[128,1,2]{2,1,0:T(1,128)S(1)}, u32[]{:S(2)}, u32[]{:S(2)}) async-start(s32[128,1,2]{2,1,0:T(1,128)} %bitcast.1), calls=%async_computation | async-start | bytes 131072 | tf_op jit(solution)/shard_map/all_to_all | solution.py:54
  15.3 0.8 convert_bitcast_fusion
  16.1 7.9 %while.42 = (s32[]{:T(128)}, f32[256,8,128]{2,1,0:T(8,128)S(1)}, s32[]{:T(128)}, s32[256]{0:T(256)}, s32[256]{0:T(256)}, /*index=5*/bf16[8,8,128]{2,1,0:T(8,128)...) while((s32[]{:T(128)}, f32[256,8,128]{2,1,0:T(8,128)S(1)}, ...), condition=%wide.region_2.4_spmd, body=%wide.region_0.3_spmd.sunk | while | flops 16975428 | bytes 3545655 | solution.py:73
  16.2 1.4 compare_and_fusion.9
  17.6 0.6 gather_fusion
  18.2 2.3 fusion.78
  20.5 0.8 dynamic_slice.71
  21.3 2.7 %scatter_fusion = f32[256,8,128]{2,1,0:T(8,128)S(1)} fusion(f32[256,8,128]{2,1,0:T(8,128)S(1)} %get-tuple-element.587, s32[64]{0:T(128)S(1)} %dynamic_slice.71, f32[64,8,128]{2,1,0:T(8,128)S(1)} %fusion.78), kind=kCustom, calls=%fused_computation.6.clone.1 | custom fusion | flops 65536 | bytes 786688 | tf_op jit(solution)/shard_map/while/body/scatter-add | solution.py:70
  24.0 1.5 copy.29
  25.6 33.3 %all-to-all-start.1 = ((f32[128,2,8,128]{3,1,2,0:T(2,128)}), f32[128,2,8,128]{3,1,2,0:T(2,128)S(1)}, u32[]{:S(2)}, u32[]{:S(2)}) async-start(f32[128,2,8,128]{3,1,2,0:T(2,128)} %copy.29), calls=%async_computation.1 | async-start | bytes 2097152 | tf_op jit(solution)/shard_map/all_to_all | solution.py:74
  58.9 0.7 reduce.7
  59.8 18.3 %all-to-all-done.1 = f32[128,2,8,128]{3,1,2,0:T(2,128)S(1)} async-done(((f32[128,2,8,128]{3,1,2,0:T(2,128)}), f32[128,2,8,128]{3,1,2,0:T(2,128)S(1)}, u32[]{:S(2)}, u32[]{:S(2)}) %all-to-all-start.1) | async-done | bytes 1048608 | tf_op jit(solution)/shard_map/all_to_all | solution.py:74
  79.0 0.8 gather_fusion.4
  79.8 1.1 broadcast_select_fusion
  80.9 4.4 %all-to-all-start.2 = ((bf16[128,2,8,128]{3,2,1,0:T(8,128)(2,1)}), bf16[128,2,8,128]{3,2,1,0:T(8,128)(2,1)S(1)}, u32[]{:S(2)}, u32[]{:S(2)}) async-start(bf16[128,2,8,128]{3,2,1,0:T(8,128)(2,1)} %bitcast.7), calls=%async_computation.2 | async-start | bytes 1048576 | tf_op jit(solution)/shard_map/all_to_all | solution.py:89
  85.4 13.7 %all-to-all-done.2 = bf16[128,2,8,128]{3,2,1,0:T(8,128)(2,1)S(1)} async-done(((bf16[128,2,8,128]{3,2,1,0:T(8,128)(2,1)}), bf16[128,2,8,128]{3,2,1,0:T(8,128)(2,1)S(1)}, u32[]{:S(2)}, u32[]{:S(2)}) %all-to-all-start.2) | async-done | bytes 524320 | tf_op jit(solution)/shard_map/all_to_all | solution.py:89
  99.1 4.6 %while.44 = (s32[]{:T(128)}, f32[8,8,128]{2,0,1:T(8,128)S(1)}, s32[]{:T(128)}, s32[256]{0:T(256)S(1)}, s32[]{:T(128)}, /*index=5*/s32[256]{0:T(256)S(1)}, bf16[2...) while((s32[]{:T(128)}, f32[8,8,128]{2,0,1:T(8,128)S(1)}, ...), condition=%wide.region_4.8_spmd.clone, body=%wide.region_3.7_spmd.clone.sunk | while | flops 23145028 | bytes 3086903 | solution.py:110
  99.1 0.7 compare_and_fusion.11
  99.8 0.6 gather_fusion.2
  100.4 2.8 %fusion.86 = f32[64,8,128]{2,1,0:T(8,128)S(1)} fusion(bf16[256,128,128]{2,1,0:T(8,128)(2,1)} %get-tuple-element.641, s32[]{:T(128)S(6)} %select_n.100, bf16[64,8,128]{2,1,0:T(8,128)(2,1)S(1)} %gather_fusion.2, pred[64]{0:T(512)(128)(4,1)S(1)} %get-tuple-element.561), kind=kOutput, calls=%fused_computation.34.clone.1 | convolution fusion | flops 16842752 | bytes 2490436 | tf_op jit(solution)/shard_map/while/body/gcf,gef->gce/dot_general | solution.py:99
  103.8 15.4 %psum.84 = f32[8]{0:T(128)S(1)} all-reduce(f32[8]{0:T(128)S(1)} %multiply_reduce_fusion.2), channel_id=1, replica_groups=mesh['rows_0'=4,'rows_1'=4,'rows_2'=4,'rows_3'=2] {'rows_0'}, use_global_device_ids=true, to_apply=%region_6.10 | all-reduce | flops 8 | bytes 64 | tf_op jit(solution)/shard_map/psum | solution.py:14
  119.2 11.4 %psum.85 = f32[8]{0:T(128)S(1)} all-reduce(f32[8]{0:T(128)S(1)} %psum.84), channel_id=1, replica_groups=mesh['rows_0'=4,'rows_1'=4,'rows_2'=4,'rows_3'=2] {'rows_1'}, use_global_device_ids=true, to_apply=%region_7.11 | all-reduce | flops 8 | bytes 64 | tf_op jit(solution)/shard_map/psum | solution.py:14
  130.5 7.3 %psum.86 = f32[8]{0:T(128)S(1)} all-reduce(f32[8]{0:T(128)S(1)} %psum.85), channel_id=1, replica_groups=mesh['rows_0'=4,'rows_1'=4,'rows_2'=4,'rows_3'=2] {'rows_2'}, use_global_device_ids=true, to_apply=%region_8.12 | all-reduce | flops 8 | bytes 64 | tf_op jit(solution)/shard_map/psum | solution.py:14
  137.8 8.3 %psum.87 = f32[8]{0:T(128)S(1)} all-reduce(f32[8]{0:T(128)S(1)} %psum.86), channel_id=1, replica_groups=mesh['rows_0'=4,'rows_1'=4,'rows_2'=4,'rows_3'=2] {'rows_3'}, use_global_device_ids=true, to_apply=%region_9.13 | all-reduce | flops 8 | bytes 64 | tf_op jit(solution)/shard_map/psum | solution.py:14
  146.3 6.5 %while.43 = (s32[]{:T(128)}, f32[256,8,128]{2,1,0:T(8,128)S(1)}, s32[]{:T(128)}, s32[256]{0:T(256)S(1)}, s32[256]{0:T(256)S(1)}, /*index=5*/bf16[8,8,128]{2,1,0:...) while((s32[]{:T(128)}, f32[256,8,128]{2,1,0:T(8,128)S(1)}, ...), condition=%wide.region_12.16_spmd, body=%wide.region_10.15_spmd.sunk | while | flops 16975428 | bytes 3545655 | solution.py:73
  146.3 0.7 compare_and_fusion.10
  147.0 0.6 gather_fusion.1
  147.7 2.3 fusion.81
  150.0 2.7 %scatter_fusion.1 = f32[256,8,128]{2,1,0:T(8,128)S(1)} fusion(f32[256,8,128]{2,1,0:T(8,128)S(1)} %get-tuple-element.659, s32[64]{0:T(128)S(1)} %dynamic_slice.73, f32[64,8,128]{2,1,0:T(8,128)S(1)} %fusion.81), kind=kCustom, calls=%fused_computation.7.clone.1 | custom fusion | flops 65536 | bytes 786688 | tf_op jit(solution)/shard_map/while/body/scatter-add | solution.py:70
  152.8 0.5 copy.33
  153.3 40.2 %all_to_all.29 = f32[128,2,8,128]{3,1,2,0:T(2,128)S(1)} all-to-all(f32[128,2,8,128]{3,1,2,0:T(2,128)S(1)} %copy.33), channel_id=1, replica_groups=mesh['rows_0'=4,'rows_1'=4,'rows_2'=4,'rows_3'=2] {'rows_0','rows_1','ro..., dimensions={0} | all-to-all | bytes 2097152 | tf_op jit(solution)/shard_map/all_to_all | solution.py:74
  193.9 0.6 multiply_reduce_fusion
  194.5 0.8 gather_fusion.5
  195.3 1.1 broadcast_select_fusion.1
  196.5 4.4 %all-to-all-start.4 = ((bf16[128,2,8,128]{3,2,1,0:T(8,128)(2,1)}), bf16[128,2,8,128]{3,2,1,0:T(8,128)(2,1)S(1)}, u32[]{:S(2)}, u32[]{:S(2)}) async-start(bf16[128,2,8,128]{3,2,1,0:T(8,128)(2,1)} %bitcast.11), calls=%async_computation.4 | async-start | bytes 1048576 | tf_op jit(solution)/shard_map/all_to_all | solution.py:89
  200.9 13.7 %all-to-all-done.4 = bf16[128,2,8,128]{3,2,1,0:T(8,128)(2,1)S(1)} async-done(((bf16[128,2,8,128]{3,2,1,0:T(8,128)(2,1)}), bf16[128,2,8,128]{3,2,1,0:T(8,128)(2,1)S(1)}, u32[]{:S(2)}, u32[]{:S(2)}) %all-to-all-start.4) | async-done | bytes 524320 | tf_op jit(solution)/shard_map/all_to_all | solution.py:89
  214.6 4.5 %while.45 = (s32[]{:T(128)}, f32[8,8,128]{2,0,1:T(8,128)S(1)}, s32[]{:T(128)}, s32[256]{0:T(256)S(1)}, s32[]{:T(128)}, /*index=5*/s32[256]{0:T(256)S(1)}, bf16[2...) while((s32[]{:T(128)}, f32[8,8,128]{2,0,1:T(8,128)S(1)}, ...), condition=%wide.region_14.18_spmd.clone, body=%wide.region_13.17_spmd.clone.sunk | while | flops 23145028 | bytes 3086903 | solution.py:110
  214.6 0.7 compare_and_fusion.12
  215.3 0.6 gather_fusion.3
  215.9 2.8 %fusion.91 = f32[64,8,128]{2,1,0:T(8,128)S(1)} fusion(bf16[256,128,128]{2,1,0:T(8,128)(2,1)} %get-tuple-element.713, s32[]{:T(128)S(6)} %select_n.102, bf16[64,8,128]{2,1,0:T(8,128)(2,1)S(1)} %gather_fusion.3, pred[64]{0:T(512)(128)(4,1)S(1)} %get-tuple-element.572), kind=kOutput, calls=%fused_computation.54.clone.1 | convolution fusion | flops 16842752 | bytes 2490436 | tf_op jit(solution)/shard_map/while/body/gcf,gef->gce/dot_general | solution.py:99
  219.3 15.4 %all-reduce.2 = (f32[8]{0:T(128)S(1)}, f32[8]{0:T(128)S(1)}) all-reduce(f32[8]{0:T(128)S(1)} %multiply_reduce_fusion.1, f32[8]{0:T(128)S(1)} %get-tuple-element.345), channel_id=1, replica_groups=mesh['rows_0'=4,'rows_1'=4,'rows_2'=4,'rows_3'=2] {'rows_0'}, use_global_device_ids=true, to_apply=%region_16.20 | all-reduce | flops 16 | bytes 128 | tf_op jit(solution)/shard_map/psum | solution.py:14
  234.7 11.4 %all-reduce.1 = (f32[8]{0:T(128)S(1)}, f32[8]{0:T(128)S(1)}) all-reduce(f32[8]{0:T(128)S(1)} %get-tuple-element.329, f32[8]{0:T(128)S(1)} %get-tuple-element.330), channel_id=1, replica_groups=mesh['rows_0'=4,'rows_1'=4,'rows_2'=4,'rows_3'=2] {'rows_1'}, use_global_device_ids=true, to_apply=%region_17.21 | all-reduce | flops 16 | bytes 128 | tf_op jit(solution)/shard_map/psum | solution.py:14
  246.0 7.3 %all-reduce = (f32[8]{0:T(128)S(1)}, f32[8]{0:T(128)S(1)}) all-reduce(f32[8]{0:T(128)S(1)} %get-tuple-element.327, f32[8]{0:T(128)S(1)} %get-tuple-element.328), channel_id=1, replica_groups=mesh['rows_0'=4,'rows_1'=4,'rows_2'=4,'rows_3'=2] {'rows_2'}, use_global_device_ids=true, to_apply=%region_18.22 | all-reduce | flops 16 | bytes 128 | tf_op jit(solution)/shard_map/psum | solution.py:14
  253.3 8.3 %all-reduce.3 = (f32[8]{0:T(128)S(1)}, f32[8]{0:T(128)S(1)}) all-reduce(f32[8]{0:T(128)S(1)} %get-tuple-element.325, f32[8]{0:T(128)S(1)} %get-tuple-element.326), channel_id=1, replica_groups=mesh['rows_0'=4,'rows_1'=4,'rows_2'=4,'rows_3'=2] {'rows_3'}, use_global_device_ids=true, to_apply=%region_19.23 | all-reduce | flops 16 | bytes 128 | tf_op jit(solution)/shard_map/psum | solution.py:14
  261.7 0.6 copy.44
  262.4 0.6 copy.45
  (36 shorter events, 3.4 us)
Async XLA Ops:
  3.1 22.4 %all-to-all-start = ((s32[128,1,2]{2,1,0:T(1,128)}), s32[128,1,2]{2,1,0:T(1,128)S(1)}, u32[]{:S(2)}, u32[]{:S(2)}) async-start(s32[128,1,2]{2,1,0:T(1,128)} %bitcast.1), calls=%async_computation | async-start | bytes 131072 | tf_op jit(solution)/shard_map/all_to_all | solution.py:54
  24.0 75.0 %copy-start = (s32[256]{0:T(256)S(1)}, s32[256]{0:T(256)}, u32[]{:S(2)}) copy-start(s32[256]{0:T(256)} %get-tuple-element.725) | copy-start | bytes 3076
  24.0 75.0 %copy-start.1 = (s32[256]{0:T(256)S(1)}, s32[256]{0:T(256)}, u32[]{:S(2)}) copy-start(s32[256]{0:T(256)} %get-tuple-element.728) | copy-start | bytes 3076
  25.6 52.5 %all-to-all-start.1 = ((f32[128,2,8,128]{3,1,2,0:T(2,128)}), f32[128,2,8,128]{3,1,2,0:T(2,128)S(1)}, u32[]{:S(2)}, u32[]{:S(2)}) async-start(f32[128,2,8,128]{3,1,2,0:T(2,128)} %copy.29), calls=%async_computation.1 | async-start | bytes 2097152 | tf_op jit(solution)/shard_map/all_to_all | solution.py:74
  80.9 18.1 %all-to-all-start.2 = ((bf16[128,2,8,128]{3,2,1,0:T(8,128)(2,1)}), bf16[128,2,8,128]{3,2,1,0:T(8,128)(2,1)S(1)}, u32[]{:S(2)}, u32[]{:S(2)}) async-start(bf16[128,2,8,128]{3,2,1,0:T(8,128)(2,1)} %bitcast.7), calls=%async_computation.2 | async-start | bytes 1048576 | tf_op jit(solution)/shard_map/all_to_all | solution.py:89
  196.5 18.1 %all-to-all-start.4 = ((bf16[128,2,8,128]{3,2,1,0:T(8,128)(2,1)}), bf16[128,2,8,128]{3,2,1,0:T(8,128)(2,1)S(1)}, u32[]{:S(2)}, u32[]{:S(2)}) async-start(bf16[128,2,8,128]{3,2,1,0:T(8,128)(2,1)} %bitcast.11), calls=%async_computation.4 | async-start | bytes 1048576 | tf_op jit(solution)/shard_map/all_to_all | solution.py:89
where the time goes:
time: 264 us; the launch traced here: 263 us
  blocking collectives  125 us (47%)
  starting transfers between devices  53.7 us (20%)
  waiting for transfers between devices  45.7 us (17%)
  other arithmetic  14.7 us (6%)
  matrix products  11.8 us (4%)
  local copies, waits for them, and re-layouts  10.8 us (4%)
    psum x8, blocking collectives, by_axis(): return functools.reduce(lax.psum, axes, x)  84.6 us
    all_to_all x1, blocking collectives, per_device(): lax.all_to_all(partial_value.reshape(devices, slots_each, columns, tile_e...  40.2 us
    all_to_all x1, starting transfers between devices, per_device(): lax.all_to_all(partial_value.reshape(devices, slots_each, columns, tile_e...  33.3 us
    all_to_all x2, waiting for transfers between devices, per_device(): lax.all_to_all(reply, ROWS, split_axis=0, concat_axis=0, tiled=True)  27.4 us
    all_to_all x1, waiting for transfers between devices, per_device(): lax.all_to_all(partial_value.reshape(devices, slots_each, columns, tile_e...  18.3 us
    all_to_all x1, starting transfers between devices, per_device(): lax.all_to_all(wanted_local.reshape(devices, slots_each), ROWS, split_axi...  11.5 us
    all_to_all x2, starting transfers between devices, per_device(): lax.all_to_all(reply, ROWS, split_axis=0, concat_axis=0, tiled=True)  8.85 us
    dot_general x2, matrix products, forward_accumulate(): jnp.einsum('gcf,gef->gce', source, tiles_now, preferred_element_type=jnp....  5.59 us
  transfers between devices with their start and end apart: 4, of which 3 were waited for; matrix products, arithmetic and copies ran while one was open for 4% of the time, Pallas kernels for 0%

commit v1 on v0

v1 whole, which is shorter than its diff:
```python
import functools

import jax
import jax.numpy as jnp
from jax import lax
from jax.experimental import pallas as pl
from jax.experimental.pallas import tpu as pltpu
from jax.sharding import PartitionSpec as P

AXIS = "rows"
EPS = 1e-06
F32 = jnp.float32
BF16 = jnp.bfloat16
CHUNKS = 8
QUADS = 8
MESH = pl.DeviceIdType.MESH


def dot_nn(lhs, rhs):
    return lax.dot_general(lhs, rhs, (((1,), (0,)), ((), ())), preferred_element_type=F32)


def dot_nt(lhs, rhs):
    return lax.dot_general(lhs, rhs, (((1,), (1,)), ((), ())), preferred_element_type=F32)


def split_bf16(x):
    high = x.astype(BF16)
    return high, (x - high.astype(F32)).astype(BF16)


def iota(shape, dim):
    return lax.broadcasted_iota(jnp.int32, shape, dim)


def kernel(
    devices,
    node_total,
    rows_s,
    slots_s,
    count_s,
    tiles_hbm,
    rows_v,
    slots_v,
    fetch_v,
    hub_v,
    hub_out,
    auth_out,
    tiles,
    prod,
    stage,
    fetched,
    onehot_slot,
    pick_t,
    pick,
    src_a,
    src_b,
    src_al,
    src_bl,
    hub_stage,
    auth_stage,
    send,
    recv,
    recv_idx,
    send_sum,
    recv_sum,
    tile_sem,
    send_sem,
    recv_sem,
    idx_send_sem,
    idx_recv_sem,
    sum_send_sem,
    sum_recv_sem,
):
    tile_total, edge, _ = tiles.shape
    cols = hub_v.shape[0]
    blocks = hub_v.shape[1] // edge
    slots_total = fetch_v.shape[1]
    slots_each = slots_total // devices
    part = slots_each * cols
    me = lax.axis_index(AXIS)
    barrier = pltpu.get_barrier_semaphore()

    per_chunk = tile_total // CHUNKS
    for q in range(CHUNKS):
        window = pl.ds(q * per_chunk, per_chunk)
        pltpu.make_async_copy(tiles_hbm.at[window], tiles.at[window], tile_sem.at[q]).start()

    @pl.loop(1, devices)
    def _(s):
        pl.semaphore_signal(
            barrier, inc=1, device_id=(lax.rem(me + s, devices),), device_id_type=MESH
        )

    zero_block = jnp.zeros((cols, edge), F32)

    def set_source(blocks_f32, with_low):
        for b in range(blocks):
            x = blocks_f32(b)
            up = jnp.concatenate([x, zero_block], axis=0)
            down = jnp.concatenate([zero_block, x], axis=0)
            if with_low:
                src_a[b], src_al[b] = split_bf16(up)
                src_b[b], src_bl[b] = split_bf16(down)
            else:
                src_a[b] = up.astype(BF16)
                src_b[b] = down.astype(BF16)

    def store_quad(t, o):
        prod[pl.ds(t, cols, stride=tile_total), :] = o[:cols, :edge]
        prod[pl.ds(t + 1, cols, stride=tile_total), :] = o[cols : 2 * cols, :edge]
        prod[pl.ds(t + 2, cols, stride=tile_total), :] = o[2 * cols : 3 * cols, edge:]
        prod[pl.ds(t + 3, cols, stride=tile_total), :] = o[3 * cols :, edge:]

    def quad_lhs(a, b, t):
        r = [rows_s[t + q] for q in range(4)]
        return jnp.concatenate(
            [
                jnp.concatenate([a[r[0]], b[r[1]]], axis=1),
                jnp.concatenate([a[r[2]], b[r[3]]], axis=1),
            ],
            axis=0,
        )

    def transpose_tiles(first, total, with_low):
        def body(i, carry):
            for u in range(QUADS):
                t = first + (i * QUADS + u) * 4
                lhs = quad_lhs(src_a, src_b, t)
                if with_low:
                    lhs = jnp.concatenate([lhs, quad_lhs(src_al, src_bl, t)], axis=0)
                rhs = jnp.concatenate(
                    [
                        tiles[pl.ds(t, 2)].reshape(2 * edge, edge),
                        tiles[pl.ds(t + 2, 2)].reshape(2 * edge, edge),
                    ],
                    axis=1,
                )
                o = dot_nn(lhs, rhs)
                if with_low:
                    o = o[: 4 * cols] + o[4 * cols :]
                store_quad(t, o)
            return carry

        lax.fori_loop(0, total // (4 * QUADS), body, 0)

    def forward_tiles():
        def body(i, carry):
            for u in range(QUADS):
                t = (i * QUADS + u) * 4
                f = [fetched[slots_s[t + q]] for q in range(4)]
                lhs = jnp.concatenate(
                    [
                        jnp.concatenate([f[0], zero_block, f[2], zero_block], axis=0),
                        jnp.concatenate([zero_block, f[1], zero_block, f[3]], axis=0),
                    ],
                    axis=1,
                ).astype(BF16)
                rhs = jnp.concatenate(
                    [
                        jnp.concatenate([tiles[t], tiles[t + 1]], axis=1),
                        jnp.concatenate([tiles[t + 2], tiles[t + 3]], axis=1),
                    ],
                    axis=0,
                )
                store_quad(t, dot_nt(lhs, rhs))
            return carry

        lax.fori_loop(0, tile_total // (4 * QUADS), body, 0)

    def prod_split(c):
        return split_bf16(prod[c * tile_total : (c + 1) * tile_total, :])

    def scatter_to_slots(phase):
        chooser = onehot_slot[...]
        for c in range(cols):
            high, low = prod_split(c)
            total = dot_nn(chooser, high) + dot_nn(chooser, low)
            stage[pl.ds(c, slots_total, stride=cols), :] = total
        send[phase] = stage[...].astype(BF16).reshape(devices, part, edge)

    def exchange_start(phase):
        @pl.loop(1, devices)
        def _(s):
            d = lax.rem(me + s, devices)
            pltpu.make_async_remote_copy(
                src_ref=send.at[phase, d],
                dst_ref=recv.at[phase, me],
                send_sem=send_sem.at[phase],
                recv_sem=recv_sem.at[phase],
                device_id=(d,),
                device_id_type=MESH,
            ).start()

        recv[phase, me] = send[phase, me]

    def wait_bytes(ref, sem):
        others = ref.at[pl.ds(0, devices - 1)]
        pltpu.make_async_copy(others, others, sem).wait()

    def exchange_wait(phase):
        wait_bytes(recv.at[phase], recv_sem.at[phase])

    def sums_start(which, row):
        send_sum[which] = row

        @pl.loop(1, devices)
        def _(s):
            d = lax.rem(me + s, devices)
            pltpu.make_async_remote_copy(
                src_ref=send_sum.at[which],
                dst_ref=recv_sum.at[which, me],
                send_sem=sum_send_sem.at[which],
                recv_sem=sum_recv_sem.at[which],
                device_id=(d,),
                device_id_type=MESH,
            ).start()

        recv_sum[which, me] = row

    def sums_wait(which):
        wait_bytes(recv_sum.at[which], sum_recv_sem.at[which])
        return jnp.sum(recv_sum[which], axis=0)

    def to_row(column, offset):
        spot = iota((cols, edge), 1) == iota((cols, edge), 0) + offset
        return jnp.sum(jnp.where(spot, column, 0.0), axis=0, keepdims=True)

    def to_column(row, offset):
        spot = iota((cols, edge), 1) == iota((cols, edge), 0) + offset
        return jnp.sum(jnp.where(spot, row, 0.0), axis=1, keepdims=True)

    def combine(phase):
        arrived = recv[phase].reshape(slots_total * cols, edge)
        return dot_nn(pick[...], arrived)

    def reply(phase, authority):
        low = authority.astype(BF16)
        low = jnp.concatenate([low, jnp.zeros_like(low)], axis=0)
        answer = dot_nn(pick_t[...], low).astype(BF16)
        send[phase] = answer.reshape(devices, part, edge)

    def gather_rows():
        alive = iota((blocks, tile_total), 1) < count_s[0]
        chooser = jnp.where(
            alive & (rows_v[...] == iota((blocks, tile_total), 0)), 1.0, 0.0
        ).astype(BF16)
        for c in range(cols):
            high, low = prod_split(c)
            total = dot_nn(chooser, high) + dot_nn(chooser, low)
            hub_stage[pl.ds(c, blocks, stride=cols), :] = total

    def column_sums(ref):
        total = jnp.zeros((cols, edge), F32)
        for b in range(blocks):
            x = ref[b * cols : (b + 1) * cols, :]
            total = total + x * x
        return jnp.sum(total, axis=1, keepdims=True)

    def spread(phase):
        arrived = recv[phase].reshape(slots_total * cols, edge)
        fetched[...] = arrived.astype(F32).reshape(slots_total, cols, edge)

    set_source(lambda b: hub_v[:, b * edge : (b + 1) * edge], False)
    alive = iota((slots_total, tile_total), 1) < count_s[0]
    onehot_slot[...] = jnp.where(
        alive & (slots_v[...] == iota((slots_total, tile_total), 0)), 1.0, 0.0
    ).astype(BF16)
    for q in range(CHUNKS):
        window = pl.ds(q * per_chunk, per_chunk)
        pltpu.make_async_copy(tiles_hbm.at[window], tiles.at[window], tile_sem.at[q]).wait()
        transpose_tiles(q * per_chunk, per_chunk, False)
    pl.semaphore_wait(barrier, devices - 1)

    @pl.loop(1, devices)
    def _(s):
        d = lax.rem(me + s, devices)
        pltpu.make_async_remote_copy(
            src_ref=fetch_v,
            dst_ref=recv_idx.at[me],
            send_sem=idx_send_sem,
            recv_sem=idx_recv_sem,
            device_id=(d,),
            device_id_type=MESH,
        ).start()

    recv_idx[me] = fetch_v[...]
    scatter_to_slots(0)
    exchange_start(0)

    wait_bytes(recv_idx, idx_recv_sem)
    lists = recv_idx[...].reshape(devices, slots_total)
    lanes = iota((devices, slots_total), 1)
    columns = [
        jnp.broadcast_to(
            jnp.sum(
                jnp.where(lanes == me * slots_each + k, lists, 0).astype(F32),
                axis=1,
                keepdims=True,
            ),
            (devices, edge),
        )
        for k in range(slots_each)
    ]
    wide = slots_total * cols
    line = jnp.zeros((cols, wide), F32)
    tall = jnp.zeros((wide, edge), F32)
    for k in range(slots_each):
        j = iota((devices, wide), 1)
        p = iota((devices, wide), 0)
        expand = jnp.where((j // part == p) & ((j // cols) % slots_each == k), 1.0, 0.0)
        line = line + dot_nn(columns[k].T[:cols].astype(BF16), expand.astype(BF16))
        j = iota((wide, devices), 0)
        p = iota((wide, devices), 1)
        expand = jnp.where((j // part == p) & ((j // cols) % slots_each == k), 1.0, 0.0)
        tall = tall + dot_nn(expand.astype(BF16), columns[k].astype(BF16))
    line_blocks = line.astype(jnp.int32)
    same = iota((cols, wide), 1) % cols == iota((cols, wide), 0)
    for b in range(0, blocks, 2):
        pick[b * cols : (b + 2) * cols, :] = jnp.concatenate(
            [jnp.where((line_blocks == b + h) & same, 1.0, 0.0) for h in range(2)], axis=0
        ).astype(BF16)
    lane = iota((wide, edge), 1)
    pick_t[...] = jnp.where(
        (tall.astype(jnp.int32) == lane // cols)
        & (iota((wide, edge), 0) % cols == lane % cols),
        1.0,
        0.0,
    ).astype(BF16)

    exchange_wait(0)
    reply(1, combine(0))
    exchange_start(1)
    exchange_wait(1)
    spread(1)
    forward_tiles()
    gather_rows()

    sums_start(0, to_row(column_sums(hub_stage), 0))
    set_source(lambda b: hub_stage[b * cols : (b + 1) * cols, :], True)
    transpose_tiles(0, tile_total, True)
    scatter_to_slots(2)
    exchange_start(2)
    scale = 1.0 / jnp.sqrt(to_column(sums_wait(0), 0) / node_total + EPS)
    exchange_wait(2)
    auth_stage[...] = combine(2) * jnp.concatenate([scale] * blocks, axis=0)
    reply(3, auth_stage[...])
    exchange_start(3)
    auth_row = to_row(column_sums(auth_stage), cols)
    exchange_wait(3)
    spread(3)
    forward_tiles()
    gather_rows()
    sums_start(1, to_row(column_sums(hub_stage), 0) + auth_row)
    totals = sums_wait(1)
    hub_scale = 1.0 / jnp.sqrt(to_column(totals, 0) / node_total + EPS)
    auth_scale = 1.0 / jnp.sqrt(to_column(totals, cols) / node_total + EPS)
    for b in range(blocks):
        here = slice(b * cols, (b + 1) * cols)
        hub_out[:, b * edge : (b + 1) * edge] = hub_stage[here, :] * hub_scale
        auth_out[:, b * edge : (b + 1) * edge] = auth_stage[here, :] * auth_scale

    wait_bytes(recv_idx, idx_send_sem)
    for which in range(2):
        wait_bytes(recv_sum.at[which], sum_send_sem.at[which])
    for phase in range(4):
        wait_bytes(recv.at[phase], send_sem.at[phase])


def per_device(edge_tiles, tile_row, tile_slot, tile_count, fetch_list, hub_start):
    devices = lax.axis_size(AXIS)
    tile_total, edge, _ = edge_tiles.shape
    cols, nodes = hub_start.shape
    blocks = nodes // edge
    slots_total = fetch_list.shape[1]
    part = slots_total // devices * cols
    smem = pl.BlockSpec(memory_space=pltpu.SMEM)
    vmem = pl.BlockSpec(memory_space=pltpu.VMEM)
    dma = pltpu.SemaphoreType.DMA
    return pl.pallas_call(
        functools.partial(kernel, devices, nodes * devices),
        out_shape=(jax.ShapeDtypeStruct((cols, nodes), F32),) * 2,
        in_specs=[smem, smem, smem, pl.BlockSpec(memory_space=pl.ANY)] + [vmem] * 4,
        out_specs=(vmem, vmem),
        scratch_shapes=[
            pltpu.VMEM((tile_total, edge, edge), BF16),
            pltpu.VMEM((cols * tile_total, edge), F32),
            pltpu.VMEM((slots_total * cols, edge), F32),
            pltpu.VMEM((slots_total, cols, edge), F32),
            pltpu.VMEM((slots_total, tile_total), BF16),
            pltpu.VMEM((slots_total * cols, edge), BF16),
            pltpu.VMEM((blocks * cols, slots_total * cols), BF16),
        ]
        + [pltpu.VMEM((blocks, 2 * cols, edge), BF16)] * 4
        + [
            pltpu.VMEM((blocks * cols, edge), F32),
            pltpu.VMEM((blocks * cols, edge), F32),
            pltpu.VMEM((4, devices, part, edge), BF16),
            pltpu.VMEM((4, devices, part, edge), BF16),
            pltpu.VMEM((devices, 1, slots_total), jnp.int32),
            pltpu.VMEM((2, 1, edge), F32),
            pltpu.VMEM((2, devices, 1, edge), F32),
            dma((CHUNKS,)),
            dma((4,)),
            dma((4,)),
            dma,
            dma,
            dma((2,)),
            dma((2,)),
        ],
        compiler_params=pltpu.CompilerParams(
            collective_id=0, has_side_effects=True, vmem_limit_bytes=60 << 20
        ),
    )(
        tile_row,
        tile_slot,
        tile_count,
        edge_tiles,
        tile_row.reshape(1, tile_total),
        tile_slot.reshape(1, tile_total),
        fetch_list,
        hub_start,
    )


def solution(mesh):
    placed = (P(AXIS, None, None), P(AXIS), P(AXIS), P(AXIS), P(AXIS, None), P(None, AXIS))
    return jax.shard_map(
        per_device,
        mesh=mesh,
        in_specs=placed,
        out_specs=(P(None, AXIS), P(None, AXIS)),
        check_vma=False,
    )
```

time: 264 us -> 76.9 us (0.29)
  blocking collectives: 125 us -> 0 us
  Pallas kernels: 0 us -> 72.5 us
  starting transfers between devices: 53.7 us -> 0 us
  waiting for transfers between devices: 45.7 us -> 0 us
  other arithmetic: 14.7 us -> 0 us
  matrix products: 11.8 us -> 0 us
  local copies, waits for them, and re-layouts: 10.8 us -> 2.75 us
    psum x8 -> x0, blocking collectives: 84.6 us -> none  [by_axis(): return functools.reduce(lax.psum, axes, x)]
    pallas_call x0 -> x1, Pallas kernels: none -> 72.5 us  [per_device(): pl.pallas_call(functools.partial(kernel, devices, nodes * devices), out_s...]
    all_to_all x4 -> x0, starting transfers between devices: 53.7 us -> none  [the longest x1 33.3 us: per_device(): lax.all_to_all(partial_value.reshape(devices, slots_each, columns, tile_e...]
    all_to_all x4 -> x0, waiting for transfers between devices: 45.7 us -> none  [the longest x2 27.4 us: per_device(): lax.all_to_all(reply, ROWS, split_axis=0, concat_axis=0, tiled=True)]
    all_to_all x1 -> x0, blocking collectives: 40.2 us -> none  [per_device(): lax.all_to_all(partial_value.reshape(devices, slots_each, columns, tile_e...]
    dot_general x8 -> x0, matrix products: 11.8 us -> none  [the longest x2 5.59 us: forward_accumulate(): jnp.einsum('gcf,gef->gce', source, tiles_now, preferred_element_type=jnp....]
    scatter-add x2 -> x0, other arithmetic: 5.47 us -> none  [transpose_accumulate(): jax.ops.segment_sum(product, slots_now, num_segments=slot_total)]
    gather x6 -> x0, local copies, waits for them, and re-layouts: 4.16 us -> none  [the longest x2 1.64 us: per_device(): jnp.take(authority_low, owner_wanted, axis=0)]
  transfers between devices with their start and end apart: 4 -> 0, of which waited for: 3 -> 0; matrix products, arithmetic and copies ran while one was open for 4% -> 0% of each run, Pallas kernels for 0% -> 0%
where the time goes in v1:
time: 76.9 us; the launch traced here: 76.6 us
  Pallas kernels  72.5 us (94%)
  local copies, waits for them, and re-layouts  2.75 us (4%)
  between operations  1.29 us (2%)
    pallas_call x1, Pallas kernels, per_device(): pl.pallas_call(functools.partial(kernel, devices, nodes * devices), out_s...  72.5 us
    unnamed x2, local copies, waits for them, and re-layouts  2.75 us

profile of v1, /device:TPU:1, one launch (start us, length us, event | category | flops | bytes accessed | tf_op | source)
XLA Modules:
  0.0 76.6 jit_solution(8890241047184636147)
XLA Ops:
  1.3 72.5 %shard_map.77 = (f32[8,1024]{1,0:T(8,128)}, f32[8,1024]{1,0:T(8,128)}) custom-call(s32[256]{0:T(256)} %rows_s.1, s32[256]{0:T(256)} %slots_s.1, s32[1]{0:T(128)S(6)} %copy.10.count_s, bf16[256,128,128]{2,1,0:T(8,128)(2,1)} %tiles_hbm.1, s32[1,256]{1,0:T(1,128)} %bitcast.2, s32[1,256]{1,0:T(1,128)} %bitcast.3, s32[1,256]{1,0:T(1,128)} %fetch_v.1, f32[8,1024]{1,0:T(8,128)} %hub_v.1), custom_call_target="tpu_custom_call" | custom-call | tf_op jit(solution)/shard_map/pallas_call | solution.py:380
  73.8 1.4 %copy.11 = f32[8,1024]{1,0:T(8,128)} copy(f32[8,1024]{1,0:T(8,128)} %get-tuple-element.4) | data formatting | bytes 65536
  75.2 1.4 %copy.12 = f32[8,1024]{1,0:T(8,128)} copy(f32[8,1024]{1,0:T(8,128)} %get-tuple-element.5) | data formatting | bytes 65536

commit v2 on v1

--- a/solution.py
+++ b/solution.py
@@ -2,6 +2,7 @@
 
 import jax
 import jax.numpy as jnp
+import numpy as np
 from jax import lax
 from jax.experimental import pallas as pl
 from jax.experimental.pallas import tpu as pltpu
@@ -11,17 +12,15 @@
 EPS = 1e-06
 F32 = jnp.float32
 BF16 = jnp.bfloat16
-CHUNKS = 8
-QUADS = 8
+CHUNKS = 4
+QUADS = 32
+TURNS = 8
+GRID = (4, 4, 4, 2)
 MESH = pl.DeviceIdType.MESH
 
 
 def dot_nn(lhs, rhs):
     return lax.dot_general(lhs, rhs, (((1,), (0,)), ((), ())), preferred_element_type=F32)
-
-
-def dot_nt(lhs, rhs):
-    return lax.dot_general(lhs, rhs, (((1,), (1,)), ((), ())), preferred_element_type=F32)
 
 
 def split_bf16(x):
@@ -31,6 +30,25 @@
 
 def iota(shape, dim):
     return lax.broadcasted_iota(jnp.int32, shape, dim)
+
+
+def ring_distance(offset):
+    return [min(o, size - o) for o, size in zip(offset[:3], GRID)]
+
+
+def send_order():
+    def key(offset):
+        away = ring_distance(offset)
+        return (-sum(d > 0 for d in away), -sum(away), offset)
+
+    every = list(np.ndindex(*GRID))[1:]
+    ordered = []
+    for offset in sorted(every, key=key):
+        back = tuple((size - o) % size for o, size in zip(offset[:3], GRID)) + offset[3:]
+        for each in (offset, back):
+            if each not in ordered:
+                ordered.append(each)
+    return ordered
 
 
 def kernel(
@@ -47,6 +65,7 @@
     hub_out,
     auth_out,
     tiles,
+    turned,
     prod,
     stage,
     fetched,
@@ -61,6 +80,7 @@
     auth_stage,
     send,
     recv,
+    send_idx,
     recv_idx,
     send_sum,
     recv_sum,
@@ -81,16 +101,26 @@
     me = lax.axis_index(AXIS)
     barrier = pltpu.get_barrier_semaphore()
 
+    order = send_order()
+    place = []
+    inner = 1
+    for size in GRID[::-1]:
+        here = lax.rem(me // inner, size)
+        place.insert(0, [lax.rem(here + k, size) * inner for k in range(size)])
+        inner *= size
+    outer_part = [[a + b for b in place[1]] for a in place[0]]
+    inner_part = [[a + b for b in place[3]] for a in place[2]]
+
+    def target(offset):
+        return outer_part[offset[0]][offset[1]] + inner_part[offset[2]][offset[3]]
+
     per_chunk = tile_total // CHUNKS
     for q in range(CHUNKS):
         window = pl.ds(q * per_chunk, per_chunk)
         pltpu.make_async_copy(tiles_hbm.at[window], tiles.at[window], tile_sem.at[q]).start()
 
-    @pl.loop(1, devices)
-    def _(s):
-        pl.semaphore_signal(
-            barrier, inc=1, device_id=(lax.rem(me + s, devices),), device_id_type=MESH
-        )
+    for offset in order:
+        pl.semaphore_signal(barrier, inc=1, device_id=(target(offset),), device_id_type=MESH)
 
     zero_block = jnp.zeros((cols, edge), F32)
 
@@ -122,27 +152,31 @@
             axis=0,
         )
 
-    def transpose_tiles(first, total, with_low):
+    def quad_rhs(ref, t):
+        return jnp.concatenate(
+            [
+                ref[pl.ds(t, 2)].reshape(2 * edge, edge),
+                ref[pl.ds(t + 2, 2)].reshape(2 * edge, edge),
+            ],
+            axis=1,
+        )
+
+    def transpose_tiles(first, total, quads, with_low, beside=None):
         def body(i, carry):
-            for u in range(QUADS):
-                t = first + (i * QUADS + u) * 4
+            if beside is not None:
+                beside(i)
+            for u in range(quads):
+                t = first + (i * quads + u) * 4
                 lhs = quad_lhs(src_a, src_b, t)
                 if with_low:
                     lhs = jnp.concatenate([lhs, quad_lhs(src_al, src_bl, t)], axis=0)
-                rhs = jnp.concatenate(
-                    [
-                        tiles[pl.ds(t, 2)].reshape(2 * edge, edge),
-                        tiles[pl.ds(t + 2, 2)].reshape(2 * edge, edge),
-                    ],
-                    axis=1,
-                )
-                o = dot_nn(lhs, rhs)
+                o = dot_nn(lhs, quad_rhs(tiles, t))
                 if with_low:
                     o = o[: 4 * cols] + o[4 * cols :]
                 store_quad(t, o)
             return carry
 
-        lax.fori_loop(0, total // (4 * QUADS), body, 0)
+        lax.fori_loop(0, total // (4 * quads), body, 0)
 
     def forward_tiles():
         def body(i, carry):
@@ -156,17 +190,19 @@
                     ],
                     axis=1,
                 ).astype(BF16)
-                rhs = jnp.concatenate(
-                    [
-                        jnp.concatenate([tiles[t], tiles[t + 1]], axis=1),
-                        jnp.concatenate([tiles[t + 2], tiles[t + 3]], axis=1),
-                    ],
-                    axis=0,
-                )
-                store_quad(t, dot_nt(lhs, rhs))
+                store_quad(t, dot_nn(lhs, quad_rhs(turned, t)))
             return carry
 
         lax.fori_loop(0, tile_total // (4 * QUADS), body, 0)
+
+    def turn_tiles():
+        def body(i, carry):
+            for u in range(TURNS):
+                t = i * TURNS + u
+                turned[t] = tiles[t].T
+            return carry
+
+        lax.fori_loop(0, tile_total // TURNS, body, 0)
 
     def prod_split(c):
         return split_bf16(prod[c * tile_total : (c + 1) * tile_total, :])
@@ -180,9 +216,8 @@
         send[phase] = stage[...].astype(BF16).reshape(devices, part, edge)
 
     def exchange_start(phase):
-        @pl.loop(1, devices)
-        def _(s):
-            d = lax.rem(me + s, devices)
+        for offset in order:
+            d = target(offset)
             pltpu.make_async_remote_copy(
                 src_ref=send.at[phase, d],
                 dst_ref=recv.at[phase, me],
@@ -201,21 +236,18 @@
     def exchange_wait(phase):
         wait_bytes(recv.at[phase], recv_sem.at[phase])
 
-    def sums_start(which, row):
+    def sums_send(which, d):
+        pltpu.make_async_remote_copy(
+            src_ref=send_sum.at[which],
+            dst_ref=recv_sum.at[which, me],
+            send_sem=sum_send_sem.at[which],
+            recv_sem=sum_recv_sem.at[which],
+            device_id=(d,),
+            device_id_type=MESH,
+        ).start()
+
+    def sums_ready(which, row):
         send_sum[which] = row
-
-        @pl.loop(1, devices)
-        def _(s):
-            d = lax.rem(me + s, devices)
-            pltpu.make_async_remote_copy(
-                src_ref=send_sum.at[which],
-                dst_ref=recv_sum.at[which, me],
-                send_sem=sum_send_sem.at[which],
-                recv_sem=sum_recv_sem.at[which],
-                device_id=(d,),
-                device_id_type=MESH,
-            ).start()
-
         recv_sum[which, me] = row
 
     def sums_wait(which):
@@ -269,39 +301,34 @@
     for q in range(CHUNKS):
         window = pl.ds(q * per_chunk, per_chunk)
         pltpu.make_async_copy(tiles_hbm.at[window], tiles.at[window], tile_sem.at[q]).wait()
-        transpose_tiles(q * per_chunk, per_chunk, False)
+        transpose_tiles(q * per_chunk, per_chunk, per_chunk // 4, False)
+    scatter_to_slots(0)
+    index = iota((slots_total, edge), 0)
+    weight = jnp.where(index % slots_each == 0, 1.0, 1.0 * blocks)
+    packer = jnp.where(index // slots_each == iota((slots_total, edge), 1), weight, 0.0)
+    list_row = jnp.broadcast_to(fetch_v[...].astype(F32), (cols, slots_total))
+    list_row = dot_nn(list_row.astype(BF16), packer.astype(BF16))[:1]
+    send_idx[...] = list_row
     pl.semaphore_wait(barrier, devices - 1)
 
-    @pl.loop(1, devices)
-    def _(s):
-        d = lax.rem(me + s, devices)
+    for offset in order:
+        d = target(offset)
         pltpu.make_async_remote_copy(
-            src_ref=fetch_v,
+            src_ref=send_idx,
             dst_ref=recv_idx.at[me],
             send_sem=idx_send_sem,
             recv_sem=idx_recv_sem,
             device_id=(d,),
             device_id_type=MESH,
         ).start()
-
-    recv_idx[me] = fetch_v[...]
-    scatter_to_slots(0)
+    recv_idx[me] = list_row
     exchange_start(0)
 
     wait_bytes(recv_idx, idx_recv_sem)
-    lists = recv_idx[...].reshape(devices, slots_total)
-    lanes = iota((devices, slots_total), 1)
-    columns = [
-        jnp.broadcast_to(
-            jnp.sum(
-                jnp.where(lanes == me * slots_each + k, lists, 0).astype(F32),
-                axis=1,
-                keepdims=True,
-            ),
-            (devices, edge),
-        )
-        for k in range(slots_each)
-    ]
+    lists = recv_idx[...].reshape(devices, edge)
+    pair = jnp.sum(jnp.where(iota((devices, edge), 1) == me, lists, 0.0), axis=1, keepdims=True)
+    pair = jnp.broadcast_to(pair, (devices, edge)).astype(jnp.int32)
+    columns = [(pair % blocks).astype(F32), (pair // blocks).astype(F32)]
     wide = slots_total * cols
     line = jnp.zeros((cols, wide), F32)
     tall = jnp.zeros((wide, edge), F32)
@@ -331,14 +358,24 @@
     exchange_wait(0)
     reply(1, combine(0))
     exchange_start(1)
+    turn_tiles()
     exchange_wait(1)
     spread(1)
     forward_tiles()
     gather_rows()
 
-    sums_start(0, to_row(column_sums(hub_stage), 0))
+    sums_ready(0, to_row(column_sums(hub_stage), 0))
     set_source(lambda b: hub_stage[b * cols : (b + 1) * cols, :], True)
-    transpose_tiles(0, tile_total, True)
+    steps = tile_total // (4 * QUADS)
+    each = devices // steps
+    for i in range(1, steps):
+        sums_send(0, lax.rem(me + i * each, devices))
+
+    def sums_beside(i):
+        for u in range(1, each):
+            sums_send(0, lax.rem(me + i * each + u, devices))
+
+    transpose_tiles(0, tile_total, QUADS, True, sums_beside)
     scatter_to_slots(2)
     exchange_start(2)
     scale = 1.0 / jnp.sqrt(to_column(sums_wait(0), 0) / node_total + EPS)
@@ -351,7 +388,9 @@
     spread(3)
     forward_tiles()
     gather_rows()
-    sums_start(1, to_row(column_sums(hub_stage), 0) + auth_row)
+    sums_ready(1, to_row(column_sums(hub_stage), 0) + auth_row)
+    for offset in order:
+        sums_send(1, target(offset))
     totals = sums_wait(1)
     hub_scale = 1.0 / jnp.sqrt(to_column(totals, 0) / node_total + EPS)
     auth_scale = 1.0 / jnp.sqrt(to_column(totals, cols) / node_total + EPS)
@@ -365,6 +404,21 @@
         wait_bytes(recv_sum.at[which], sum_send_sem.at[which])
     for phase in range(4):
         wait_bytes(recv.at[phase], send_sem.at[phase])
+
+
+def finish_kernel(hub_in, auth_in, hub_out, auth_out):
+    hub_out[...] = hub_in[...]
+    auth_out[...] = auth_in[...]
+
+
+def finish(hub, authority):
+    vmem = pl.BlockSpec(memory_space=pltpu.VMEM)
+    return pl.pallas_call(
+        finish_kernel,
+        out_shape=(jax.ShapeDtypeStruct(hub.shape, F32),) * 2,
+        in_specs=[vmem] * 2,
+        out_specs=(vmem, vmem),
+    )(hub, authority)
 
 
 def per_device(edge_tiles, tile_row, tile_slot, tile_count, fetch_list, hub_start):
@@ -377,12 +431,13 @@
     smem = pl.BlockSpec(memory_space=pltpu.SMEM)
     vmem = pl.BlockSpec(memory_space=pltpu.VMEM)
     dma = pltpu.SemaphoreType.DMA
-    return pl.pallas_call(
+    results = pl.pallas_call(
         functools.partial(kernel, devices, nodes * devices),
         out_shape=(jax.ShapeDtypeStruct((cols, nodes), F32),) * 2,
         in_specs=[smem, smem, smem, pl.BlockSpec(memory_space=pl.ANY)] + [vmem] * 4,
         out_specs=(vmem, vmem),
         scratch_shapes=[
+            pltpu.VMEM((tile_total, edge, edge), BF16),
             pltpu.VMEM((tile_total, edge, edge), BF16),
             pltpu.VMEM((cols * tile_total, edge), F32),
             pltpu.VMEM((slots_total * cols, edge), F32),
@@ -397,7 +452,8 @@
             pltpu.VMEM((blocks * cols, edge), F32),
             pltpu.VMEM((4, devices, part, edge), BF16),
             pltpu.VMEM((4, devices, part, edge), BF16),
-            pltpu.VMEM((devices, 1, slots_total), jnp.int32),
+            pltpu.VMEM((1, edge), F32),
+            pltpu.VMEM((devices, 1, edge), F32),
             pltpu.VMEM((2, 1, edge), F32),
             pltpu.VMEM((2, devices, 1, edge), F32),
             dma((CHUNKS,)),
@@ -421,6 +477,7 @@
         fetch_list,
         hub_start,
     )
+    return finish(*results)
 
 
 def solution(mesh):

time: 76.9 us -> 65.7 us (0.85)
  Pallas kernels: 72.5 us -> 64.1 us
  local copies, waits for them, and re-layouts: 2.75 us -> 0 us
    pallas_call x1, Pallas kernels: 72.5 us -> 62.7 us  [per_device(): pl.pallas_call(functools.partial(kernel, devices, nodes * devices), out_s...]
    unnamed x2 -> x0, local copies, waits for them, and re-layouts: 2.75 us -> none
    pallas_call x0 -> x1, Pallas kernels: none -> 1.4 us  [finish(): pl.pallas_call(finish_kernel, out_shape=(jax.ShapeDtypeStruct(hub.shape,...]
where the time goes in v2:
time: 65.7 us; the launch traced here: 65.4 us
  Pallas kernels  64.1 us (98%)
  between operations  1.29 us (2%)
    pallas_call x1, Pallas kernels, per_device(): pl.pallas_call(functools.partial(kernel, devices, nodes * devices), out_s...  62.7 us
    pallas_call x1, Pallas kernels, finish(): pl.pallas_call(finish_kernel, out_shape=(jax.ShapeDtypeStruct(hub.shape,...  1.4 us

profile of v2, /device:TPU:1, one launch (start us, length us, event | category | flops | bytes accessed | tf_op | source)
XLA Modules:
  0.0 65.4 jit_solution(12842427435537598201)
XLA Ops:
  1.3 62.7 %shard_map.77 = (f32[8,1024]{1,0:T(8,128)}, f32[8,1024]{1,0:T(8,128)}) custom-call(s32[256]{0:T(256)} %rows_s.1, s32[256]{0:T(256)} %slots_s.1, s32[1]{0:T(128)S(6)} %copy.8.count_s, bf16[256,128,128]{2,1,0:T(8,128)(2,1)} %tiles_hbm.1, s32[1,256]{1,0:T(1,128)} %bitcast.2, s32[1,256]{1,0:T(1,128)} %bitcast.3, s32[1,256]{1,0:T(1,128)} %fetch_v.1, f32[8,1024]{1,0:T(8,128)} %hub_v.1), custom_call_target="tpu_custom_call" | custom-call | tf_op jit(solution)/shard_map/pallas_call | solution.py:434
  64.0 1.4 %shard_map.78 = (f32[8,1024]{1,0:T(8,128)}, f32[8,1024]{1,0:T(8,128)}) custom-call(f32[8,1024]{1,0:T(8,128)} %get-tuple-element.4.hub_in, f32[8,1024]{1,0:T(8,128)} %get-tuple-element.5.auth_in), custom_call_target="tpu_custom_call" | custom-call | tf_op jit(solution)/shard_map/pallas_call | solution.py:416

commit v3 on v2

--- a/solution.py
+++ b/solution.py
@@ -15,6 +15,7 @@
 CHUNKS = 4
 QUADS = 32
 TURNS = 8
+HALVES = 2
 GRID = (4, 4, 4, 2)
 MESH = pl.DeviceIdType.MESH
 
@@ -97,7 +98,9 @@
     blocks = hub_v.shape[1] // edge
     slots_total = fetch_v.shape[1]
     slots_each = slots_total // devices
-    part = slots_each * cols
+    half = cols // HALVES
+    part = slots_each * half
+    wide = slots_total * half
     me = lax.axis_index(AXIS)
     barrier = pltpu.get_barrier_semaphore()
 
@@ -207,34 +210,33 @@
     def prod_split(c):
         return split_bf16(prod[c * tile_total : (c + 1) * tile_total, :])
 
-    def scatter_to_slots(phase):
+    def scatter_to_slots(phase, h):
         chooser = onehot_slot[...]
-        for c in range(cols):
-            high, low = prod_split(c)
+        for c in range(half):
+            high, low = prod_split(h * half + c)
             total = dot_nn(chooser, high) + dot_nn(chooser, low)
-            stage[pl.ds(c, slots_total, stride=cols), :] = total
-        send[phase] = stage[...].astype(BF16).reshape(devices, part, edge)
-
-    def exchange_start(phase):
+            stage[h, pl.ds(c, slots_total, stride=half), :] = total
+        send[phase, h] = stage[h].astype(BF16).reshape(devices, part, edge)
+
+    def exchange_start(phase, h):
         for offset in order:
             d = target(offset)
             pltpu.make_async_remote_copy(
-                src_ref=send.at[phase, d],
-                dst_ref=recv.at[phase, me],
-                send_sem=send_sem.at[phase],
-                recv_sem=recv_sem.at[phase],
+                src_ref=send.at[phase, h, d],
+                dst_ref=recv.at[phase, h, me],
+                send_sem=send_sem.at[phase, h],
+                recv_sem=recv_sem.at[phase, h],
                 device_id=(d,),
                 device_id_type=MESH,
             ).start()
-
-        recv[phase, me] = send[phase, me]
+        recv[phase, h, me] = send[phase, h, me]
 
     def wait_bytes(ref, sem):
         others = ref.at[pl.ds(0, devices - 1)]
         pltpu.make_async_copy(others, others, sem).wait()
 
-    def exchange_wait(phase):
-        wait_bytes(recv.at[phase], recv_sem.at[phase])
+    def exchange_wait(phase, h):
+        wait_bytes(recv.at[phase, h], recv_sem.at[phase, h])
 
     def sums_send(which, d):
         pltpu.make_async_remote_copy(
@@ -254,23 +256,25 @@
         wait_bytes(recv_sum.at[which], sum_recv_sem.at[which])
         return jnp.sum(recv_sum[which], axis=0)
 
-    def to_row(column, offset):
-        spot = iota((cols, edge), 1) == iota((cols, edge), 0) + offset
+    def to_row(column, offset, period):
+        spot = iota((cols, edge), 1) == iota((cols, edge), 0) % period + offset
         return jnp.sum(jnp.where(spot, column, 0.0), axis=0, keepdims=True)
 
-    def to_column(row, offset):
-        spot = iota((cols, edge), 1) == iota((cols, edge), 0) + offset
+    def to_column(row, offset, period):
+        spot = iota((cols, edge), 1) == iota((cols, edge), 0) % period + offset
         return jnp.sum(jnp.where(spot, row, 0.0), axis=1, keepdims=True)
 
-    def combine(phase):
-        arrived = recv[phase].reshape(slots_total * cols, edge)
-        return dot_nn(pick[...], arrived)
-
-    def reply(phase, authority):
+    def inverse_norm(row, offset, period):
+        return 1.0 / jnp.sqrt(to_column(row, offset, period) / node_total + EPS)
+
+    def combine(phase, h):
+        return dot_nn(pick[...], recv[phase, h].reshape(wide, edge))
+
+    def reply(phase, h, authority):
         low = authority.astype(BF16)
-        low = jnp.concatenate([low, jnp.zeros_like(low)], axis=0)
+        low = jnp.concatenate([low, jnp.zeros((edge - blocks * half, edge), BF16)], axis=0)
         answer = dot_nn(pick_t[...], low).astype(BF16)
-        send[phase] = answer.reshape(devices, part, edge)
+        send[phase, h] = answer.reshape(devices, part, edge)
 
     def gather_rows():
         alive = iota((blocks, tile_total), 1) < count_s[0]
@@ -284,14 +288,14 @@
 
     def column_sums(ref):
         total = jnp.zeros((cols, edge), F32)
-        for b in range(blocks):
-            x = ref[b * cols : (b + 1) * cols, :]
+        for g in range(ref.shape[0] // cols):
+            x = ref[g * cols : (g + 1) * cols, :]
             total = total + x * x
         return jnp.sum(total, axis=1, keepdims=True)
 
-    def spread(phase):
-        arrived = recv[phase].reshape(slots_total * cols, edge)
-        fetched[...] = arrived.astype(F32).reshape(slots_total, cols, edge)
+    def spread(phase, h):
+        arrived = recv[phase, h].reshape(wide, edge).astype(F32)
+        fetched[:, h * half : (h + 1) * half, :] = arrived.reshape(slots_total, half, edge)
 
     set_source(lambda b: hub_v[:, b * edge : (b + 1) * edge], False)
     alive = iota((slots_total, tile_total), 1) < count_s[0]
@@ -302,7 +306,8 @@
         window = pl.ds(q * per_chunk, per_chunk)
         pltpu.make_async_copy(tiles_hbm.at[window], tiles.at[window], tile_sem.at[q]).wait()
         transpose_tiles(q * per_chunk, per_chunk, per_chunk // 4, False)
-    scatter_to_slots(0)
+    for h in range(HALVES):
+        scatter_to_slots(0, h)
     index = iota((slots_total, edge), 0)
     weight = jnp.where(index % slots_each == 0, 1.0, 1.0 * blocks)
     packer = jnp.where(index // slots_each == iota((slots_total, edge), 1), weight, 0.0)
@@ -322,49 +327,56 @@
             device_id_type=MESH,
         ).start()
     recv_idx[me] = list_row
-    exchange_start(0)
+    for h in range(HALVES):
+        exchange_start(0, h)
 
     wait_bytes(recv_idx, idx_recv_sem)
     lists = recv_idx[...].reshape(devices, edge)
     pair = jnp.sum(jnp.where(iota((devices, edge), 1) == me, lists, 0.0), axis=1, keepdims=True)
     pair = jnp.broadcast_to(pair, (devices, edge)).astype(jnp.int32)
     columns = [(pair % blocks).astype(F32), (pair // blocks).astype(F32)]
-    wide = slots_total * cols
     line = jnp.zeros((cols, wide), F32)
     tall = jnp.zeros((wide, edge), F32)
     for k in range(slots_each):
         j = iota((devices, wide), 1)
         p = iota((devices, wide), 0)
-        expand = jnp.where((j // part == p) & ((j // cols) % slots_each == k), 1.0, 0.0)
+        expand = jnp.where((j // part == p) & ((j // half) % slots_each == k), 1.0, 0.0)
         line = line + dot_nn(columns[k].T[:cols].astype(BF16), expand.astype(BF16))
         j = iota((wide, devices), 0)
         p = iota((wide, devices), 1)
-        expand = jnp.where((j // part == p) & ((j // cols) % slots_each == k), 1.0, 0.0)
+        expand = jnp.where((j // part == p) & ((j // half) % slots_each == k), 1.0, 0.0)
         tall = tall + dot_nn(expand.astype(BF16), columns[k].astype(BF16))
     line_blocks = line.astype(jnp.int32)
-    same = iota((cols, wide), 1) % cols == iota((cols, wide), 0)
-    for b in range(0, blocks, 2):
-        pick[b * cols : (b + 2) * cols, :] = jnp.concatenate(
-            [jnp.where((line_blocks == b + h) & same, 1.0, 0.0) for h in range(2)], axis=0
+    row = iota((cols, wide), 0)
+    same = iota((cols, wide), 1) % half == row % half
+    for b in range(0, blocks, 4):
+        pick[b * half : (b + 4) * half, :] = jnp.concatenate(
+            [
+                jnp.where((line_blocks == b + g + row // half) & same, 1.0, 0.0)
+                for g in range(0, 4, cols // half)
+            ],
+            axis=0,
         ).astype(BF16)
     lane = iota((wide, edge), 1)
     pick_t[...] = jnp.where(
-        (tall.astype(jnp.int32) == lane // cols)
-        & (iota((wide, edge), 0) % cols == lane % cols),
+        (tall.astype(jnp.int32) == lane // half)
+        & (iota((wide, edge), 0) % half == lane % half),
         1.0,
         0.0,
     ).astype(BF16)
 
-    exchange_wait(0)
-    reply(1, combine(0))
-    exchange_start(1)
+    for h in range(HALVES):
+        exchange_wait(0, h)
+        reply(1, h, combine(0, h))
+        exchange_start(1, h)
     turn_tiles()
-    exchange_wait(1)
-    spread(1)
+    for h in range(HALVES):
+        exchange_wait(1, h)
+        spread(1, h)
     forward_tiles()
     gather_rows()
 
-    sums_ready(0, to_row(column_sums(hub_stage), 0))
+    sums_ready(0, to_row(column_sums(hub_stage), 0, cols))
     set_source(lambda b: hub_stage[b * cols : (b + 1) * cols, :], True)
     steps = tile_total // (4 * QUADS)
     each = devices // steps
@@ -376,34 +388,46 @@
             sums_send(0, lax.rem(me + i * each + u, devices))
 
     transpose_tiles(0, tile_total, QUADS, True, sums_beside)
-    scatter_to_slots(2)
-    exchange_start(2)
-    scale = 1.0 / jnp.sqrt(to_column(sums_wait(0), 0) / node_total + EPS)
-    exchange_wait(2)
-    auth_stage[...] = combine(2) * jnp.concatenate([scale] * blocks, axis=0)
-    reply(3, auth_stage[...])
-    exchange_start(3)
-    auth_row = to_row(column_sums(auth_stage), cols)
-    exchange_wait(3)
-    spread(3)
+    for h in range(HALVES):
+        scatter_to_slots(2, h)
+        exchange_start(2, h)
+    totals = sums_wait(0)
+    auth_row = jnp.zeros((1, edge), F32)
+    for h in range(HALVES):
+        scale = inverse_norm(totals, h * half, half)
+        exchange_wait(2, h)
+        auth_stage[h] = combine(2, h) * jnp.concatenate([scale] * (blocks * half // cols), axis=0)
+        reply(3, h, auth_stage[h])
+        exchange_start(3, h)
+        auth_row += to_row(column_sums(auth_stage.at[h]), cols + h * half, half)
+    for h in range(HALVES):
+        exchange_wait(3, h)
+        spread(3, h)
     forward_tiles()
     gather_rows()
-    sums_ready(1, to_row(column_sums(hub_stage), 0) + auth_row)
+    sums_ready(1, to_row(column_sums(hub_stage), 0, cols) + auth_row)
     for offset in order:
         sums_send(1, target(offset))
     totals = sums_wait(1)
-    hub_scale = 1.0 / jnp.sqrt(to_column(totals, 0) / node_total + EPS)
-    auth_scale = 1.0 / jnp.sqrt(to_column(totals, cols) / node_total + EPS)
+    hub_scale = inverse_norm(totals, 0, cols)
     for b in range(blocks):
-        here = slice(b * cols, (b + 1) * cols)
-        hub_out[:, b * edge : (b + 1) * edge] = hub_stage[here, :] * hub_scale
-        auth_out[:, b * edge : (b + 1) * edge] = auth_stage[here, :] * auth_scale
+        hub_out[:, b * edge : (b + 1) * edge] = hub_stage[b * cols : (b + 1) * cols, :] * hub_scale
+    for h in range(HALVES):
+        auth_scale = inverse_norm(totals, cols + h * half, half)
+        for g in range(blocks * half // cols):
+            both = auth_stage[h, g * cols : (g + 1) * cols, :] * auth_scale
+            for q in range(cols // half):
+                b = g * (cols // half) + q
+                auth_out[h * half : (h + 1) * half, b * edge : (b + 1) * edge] = both[
+                    q * half : (q + 1) * half
+                ]
 
     wait_bytes(recv_idx, idx_send_sem)
     for which in range(2):
         wait_bytes(recv_sum.at[which], sum_send_sem.at[which])
     for phase in range(4):
-        wait_bytes(recv.at[phase], send_sem.at[phase])
+        for h in range(HALVES):
+            wait_bytes(recv.at[phase, h], send_sem.at[phase, h])
 
 
 def finish_kernel(hub_in, auth_in, hub_out, auth_out):
@@ -427,7 +451,9 @@
     cols, nodes = hub_start.shape
     blocks = nodes // edge
     slots_total = fetch_list.shape[1]
-    part = slots_total // devices * cols
+    half = cols // HALVES
+    part = slots_total // devices * half
+    wide = slots_total * half
     smem = pl.BlockSpec(memory_space=pltpu.SMEM)
     vmem = pl.BlockSpec(memory_space=pltpu.VMEM)
     dma = pltpu.SemaphoreType.DMA
@@ -440,25 +466,25 @@
             pltpu.VMEM((tile_total, edge, edge), BF16),
             pltpu.VMEM((tile_total, edge, edge), BF16),
             pltpu.VMEM((cols * tile_total, edge), F32),
-            pltpu.VMEM((slots_total * cols, edge), F32),
+            pltpu.VMEM((HALVES, wide, edge), F32),
             pltpu.VMEM((slots_total, cols, edge), F32),
             pltpu.VMEM((slots_total, tile_total), BF16),
-            pltpu.VMEM((slots_total * cols, edge), BF16),
-            pltpu.VMEM((blocks * cols, slots_total * cols), BF16),
+            pltpu.VMEM((wide, edge), BF16),
+            pltpu.VMEM((blocks * half, wide), BF16),
         ]
         + [pltpu.VMEM((blocks, 2 * cols, edge), BF16)] * 4
         + [
             pltpu.VMEM((blocks * cols, edge), F32),
-            pltpu.VMEM((blocks * cols, edge), F32),
-            pltpu.VMEM((4, devices, part, edge), BF16),
-            pltpu.VMEM((4, devices, part, edge), BF16),
+            pltpu.VMEM((HALVES, blocks * half, edge), F32),
+            pltpu.VMEM((4, HALVES, devices, part, edge), BF16),
+            pltpu.VMEM((4, HALVES, devices, part, edge), BF16),
             pltpu.VMEM((1, edge), F32),
             pltpu.VMEM((devices, 1, edge), F32),
             pltpu.VMEM((2, 1, edge), F32),
             pltpu.VMEM((2, devices, 1, edge), F32),
             dma((CHUNKS,)),
-            dma((4,)),
-            dma((4,)),
+            dma((4, HALVES)),
+            dma((4, HALVES)),
             dma,
             dma,
             dma((2,)),

time: 65.7 us -> 62 us (0.944)
  Pallas kernels: 64.1 us -> 60.6 us
    pallas_call x1, Pallas kernels: 62.7 us -> 59.2 us  [per_device(): pl.pallas_call(functools.partial(kernel, devices, nodes * devices), out_s...]
where the time goes in v3:
time: 62 us; the launch traced here: 61.9 us
  Pallas kernels  60.6 us (98%)
  between operations  1.29 us (2%)
    pallas_call x1, Pallas kernels, per_device(): pl.pallas_call(functools.partial(kernel, devices, nodes * devices), out_s...  59.2 us
    pallas_call x1, Pallas kernels, finish(): pl.pallas_call(finish_kernel, out_shape=(jax.ShapeDtypeStruct(hub.shape,...  1.4 us

profile of v3, /device:TPU:1, one launch (start us, length us, event | category | flops | bytes accessed | tf_op | source)
XLA Modules:
  0.0 61.9 jit_solution(2349840841345843300)
XLA Ops:
  1.3 59.2 %shard_map.77 = (f32[8,1024]{1,0:T(8,128)}, f32[8,1024]{1,0:T(8,128)}) custom-call(s32[256]{0:T(256)} %rows_s.1, s32[256]{0:T(256)} %slots_s.1, s32[1]{0:T(128)S(6)} %copy.8.count_s, bf16[256,128,128]{2,1,0:T(8,128)(2,1)} %tiles_hbm.1, s32[1,256]{1,0:T(1,128)} %bitcast.2, s32[1,256]{1,0:T(1,128)} %bitcast.3, s32[1,256]{1,0:T(1,128)} %fetch_v.1, f32[8,1024]{1,0:T(8,128)} %hub_v.1), custom_call_target="tpu_custom_call" | custom-call | tf_op jit(solution)/shard_map/pallas_call | solution.py:460
  60.5 1.4 %shard_map.78 = (f32[8,1024]{1,0:T(8,128)}, f32[8,1024]{1,0:T(8,128)}) custom-call(f32[8,1024]{1,0:T(8,128)} %get-tuple-element.4.hub_in, f32[8,1024]{1,0:T(8,128)} %get-tuple-element.5.auth_in), custom_call_target="tpu_custom_call" | custom-call | tf_op jit(solution)/shard_map/pallas_call | solution.py:440

commit v4 on v3

--- a/solution.py
+++ b/solution.py
@@ -13,9 +13,9 @@
 F32 = jnp.float32
 BF16 = jnp.bfloat16
 CHUNKS = 4
-QUADS = 32
+QUADS = 64
 TURNS = 8
-HALVES = 2
+HALVES = 4
 GRID = (4, 4, 4, 2)
 MESH = pl.DeviceIdType.MESH
 
@@ -442,7 +442,7 @@
         out_shape=(jax.ShapeDtypeStruct(hub.shape, F32),) * 2,
         in_specs=[vmem] * 2,
         out_specs=(vmem, vmem),
-    )(hub, authority)
+    )(*[pltpu.with_memory_space_constraint(v, pltpu.VMEM) for v in (hub, authority)])
 
 
 def per_device(edge_tiles, tile_row, tile_slot, tile_count, fetch_list, hub_start):
@@ -459,7 +459,7 @@
     dma = pltpu.SemaphoreType.DMA
     results = pl.pallas_call(
         functools.partial(kernel, devices, nodes * devices),
-        out_shape=(jax.ShapeDtypeStruct((cols, nodes), F32),) * 2,
+        out_shape=(pltpu.VMEM((cols, nodes), F32),) * 2,
         in_specs=[smem, smem, smem, pl.BlockSpec(memory_space=pl.ANY)] + [vmem] * 4,
         out_specs=(vmem, vmem),
         scratch_shapes=[

time: 62 us -> 59.3 us (0.956)
  Pallas kernels: 60.6 us -> 57.8 us
    pallas_call x1, Pallas kernels: 59.2 us -> 57.1 us  [per_device(): pl.pallas_call(functools.partial(kernel, devices, nodes * devices), out_s...]
    pallas_call x1, Pallas kernels: 1.4 us -> 0.63 us  [finish(): pl.pallas_call(finish_kernel, out_shape=(jax.ShapeDtypeStruct(hub.shape,...]
where the time goes in v4:
time: 59.3 us; the launch traced here: 59.1 us
  Pallas kernels  57.8 us (97%)
  between operations  1.29 us (2%)
    pallas_call x1, Pallas kernels, per_device(): pl.pallas_call(functools.partial(kernel, devices, nodes * devices), out_s...  57.1 us

profile of v4, /device:TPU:1, one launch (start us, length us, event | category | flops | bytes accessed | tf_op | source)
XLA Modules:
  0.0 59.1 jit_solution(16452319694897861532)
XLA Ops:
  1.3 57.1 %shard_map.77 = (f32[8,1024]{1,0:T(8,128)S(1)}, f32[8,1024]{1,0:T(8,128)S(1)}) custom-call(s32[256]{0:T(256)} %rows_s.1, s32[256]{0:T(256)} %slots_s.1, s32[1]{0:T(128)S(6)} %copy.8.count_s, bf16[256,128,128]{2,1,0:T(8,128)(2,1)} %tiles_hbm.1, s32[1,256]{1,0:T(1,128)} %bitcast.2, s32[1,256]{1,0:T(1,128)} %bitcast.3, s32[1,256]{1,0:T(1,128)} %fetch_v.1, ...), custom_call_target="tpu_custom_call" | custom-call | tf_op jit(solution)/shard_map/pallas_call | solution.py:460
  58.4 0.6 %shard_map.78 = (f32[8,1024]{1,0:T(8,128)}, f32[8,1024]{1,0:T(8,128)}) custom-call(f32[8,1024]{1,0:T(8,128)S(1)} %get-tuple-element.4.hub_in, f32[8,1024]{1,0:T(8,128)S(1)} %get-tuple-element.5.auth_in), custom_call_target="tpu_custom_call" | custom-call | tf_op jit(solution)/shard_map/pallas_call | solution.py:440

commit v5 on v4

--- a/solution.py
+++ b/solution.py
@@ -12,9 +12,9 @@
 EPS = 1e-06
 F32 = jnp.float32
 BF16 = jnp.bfloat16
-CHUNKS = 4
+CHUNKS = 8
 QUADS = 64
-TURNS = 8
+TURNS = 16
 HALVES = 4
 GRID = (4, 4, 4, 2)
 MESH = pl.DeviceIdType.MESH
@@ -214,7 +214,8 @@
         chooser = onehot_slot[...]
         for c in range(half):
             high, low = prod_split(h * half + c)
-            total = dot_nn(chooser, high) + dot_nn(chooser, low)
+            total = dot_nn(chooser, jnp.concatenate([high, low], axis=1))
+            total = total[:, :edge] + total[:, edge:]
             stage[h, pl.ds(c, slots_total, stride=half), :] = total
         send[phase, h] = stage[h].astype(BF16).reshape(devices, part, edge)
 

time: 59.3 us -> 58.6 us (0.988)
  Pallas kernels: 57.8 us -> 57.1 us
    pallas_call x1, Pallas kernels: 57.1 us -> 56.5 us  [per_device(): pl.pallas_call(functools.partial(kernel, devices, nodes * devices), out_s...]
where the time goes in v5:
time: 58.6 us; the launch traced here: 58.4 us
  Pallas kernels  57.1 us (97%)
  between operations  1.29 us (2%)
    pallas_call x1, Pallas kernels, per_device(): pl.pallas_call(functools.partial(kernel, devices, nodes * devices), out_s...  56.5 us

profile of v5, /device:TPU:1, one launch (start us, length us, event | category | flops | bytes accessed | tf_op | source)
XLA Modules:
  0.0 58.4 jit_solution(3566947692300662335)
XLA Ops:
  1.3 56.5 %shard_map.77 = (f32[8,1024]{1,0:T(8,128)S(1)}, f32[8,1024]{1,0:T(8,128)S(1)}) custom-call(s32[256]{0:T(256)} %rows_s.1, s32[256]{0:T(256)} %slots_s.1, s32[1]{0:T(128)S(6)} %copy.8.count_s, bf16[256,128,128]{2,1,0:T(8,128)(2,1)} %tiles_hbm.1, s32[1,256]{1,0:T(1,128)} %bitcast.2, s32[1,256]{1,0:T(1,128)} %bitcast.3, s32[1,256]{1,0:T(1,128)} %fetch_v.1, ...), custom_call_target="tpu_custom_call" | custom-call | tf_op jit(solution)/shard_map/pallas_call | solution.py:461
  57.8 0.6 %shard_map.78 = (f32[8,1024]{1,0:T(8,128)}, f32[8,1024]{1,0:T(8,128)}) custom-call(f32[8,1024]{1,0:T(8,128)S(1)} %get-tuple-element.4.hub_in, f32[8,1024]{1,0:T(8,128)S(1)} %get-tuple-element.5.auth_in), custom_call_target="tpu_custom_call" | custom-call | tf_op jit(solution)/shard_map/pallas_call | solution.py:441
